TPU v7x, 32 devices: a whole 2x2x4 slice. The times are simulated.
32 devices in a mesh: mem: 4 (over x, core), grid: 8 (over z, y).
Axes of the slice: x: 2, y: 2, z: 4, core: 2. Of those that a mesh axis runs over, the one named last changes fastest.
Arguments:
- obs_ensemble: bfloat16 [256, 32, 256], P('mem', 'grid'), may hold values from -6 to 6
- obs_values: bfloat16 [32, 256], P('grid'), may hold values from -6 to 6
- inverse_error: bfloat16 [32, 256], P('grid'), may hold values from 0.5 to 8
- obs_counts: int32 [32], P('grid'), may hold values from 1 to 256, as said below
- loc_offsets: int32 [32, 4], P('grid'), may hold values from -2 to 2, as said below
- background: bfloat16 [256, 256, 320], P('mem', 'grid'), may hold values from -6 to 6
Outputs:
- analysis: bfloat16 [256, 256, 320], P('mem', 'grid')
Inputs may be any that keep to these rules, and one draw needn't show every extreme that they name: `obs_counts`: counts up to about five times their mean; some block in every draw is full. `loc_offsets`: entry 0 of every list is 0 (the block's own observations); the other entries of a list are distinct nonzero offsets.
All inputs are finite; a program needn't handle non-finite values.
Results may differ from a plain program's by a relative error of at most 0.0063.
Values may be sent and summed in bfloat16 or wider, within the bound.
A program may use at most 128 MiB of HBM per device.

v0:
```python
import jax
import jax.numpy as jnp
from jax import lax
from jax.sharding import PartitionSpec as P

MEMBERS = 256
BLOCK_COLS = 8
REACH = 2
LOC_LEN = 4
NS_STEPS = 6


def padded(x, sides, width):
    for axis, dim in sides:
        count, length = (lax.axis_size(axis), x.shape[dim])
        up = [(i, (i + 1) % count) for i in range(count)]
        down = [(j, i) for i, j in up]
        last = lax.slice_in_dim(x, length - width, length, axis=dim)
        initial = lax.slice_in_dim(x, 0, width, axis=dim)
        before = lax.ppermute(last, axis, up)
        after = lax.ppermute(initial, axis, down)
        x = jnp.concatenate([before, x, after], axis=dim)
    return x


def taper_of(offsets):
    return 1.0 / (1.0 + jnp.abs(offsets).astype(jnp.float32))


def block_weights(members, obs_row, weight_row):
    members_wide = members.astype(jnp.float32)
    obs_mean = jnp.mean(members_wide, axis=0)
    scaled = ((members_wide - obs_mean) * weight_row).astype(jnp.bfloat16)
    innovation = (obs_row - obs_mean) * weight_row
    gram = jnp.dot(scaled, scaled.T, preferred_element_type=jnp.float32)
    rhs = jnp.dot(scaled.astype(jnp.float32), innovation, precision=lax.Precision.HIGHEST)
    identity = jnp.eye(MEMBERS, dtype=jnp.float32)
    system = identity + gram / (MEMBERS - 1)
    scale = jnp.sqrt(jnp.sum(system * system))
    upper = system / scale
    lower = identity
    for step in range(NS_STEPS):
        middle = 0.5 * (3.0 * identity - jnp.dot(lower, upper, precision=lax.Precision.HIGHEST))
        upper = jnp.dot(upper, middle, precision=lax.Precision.HIGHEST)
        lower = jnp.dot(middle, lower, precision=lax.Precision.HIGHEST)
    root_inv = lower / jnp.sqrt(scale)
    inner = jnp.dot(root_inv, rhs, precision=lax.Precision.HIGHEST)
    shift = jnp.dot(root_inv, inner, precision=lax.Precision.HIGHEST) / (MEMBERS - 1)
    return (root_inv + shift[:, None]).astype(jnp.bfloat16)


def apply_weights(weights, state):
    state_wide = state.astype(jnp.float32)
    state_mean = jnp.mean(state_wide, axis=0)
    perturbation = (state_wide - state_mean).astype(jnp.bfloat16)
    product = jnp.einsum("bkj,kbv->jbv", weights, perturbation, preferred_element_type=jnp.float32)
    return (state_mean + product).astype(jnp.bfloat16)


def on_device(obs_ensemble, obs_values, inverse_error, obs_counts, loc_offsets, background):
    local_members, dev_blocks, slots = obs_ensemble.shape
    mem_count = lax.axis_size("mem")
    per_device = dev_blocks // mem_count
    list_width = LOC_LEN * slots
    slot_ids = jnp.arange(slots, dtype=jnp.int32)
    valid = (slot_ids[None, :] < obs_counts[:, None]).astype(jnp.float32)
    masked = (inverse_error.astype(jnp.float32) * valid).astype(jnp.bfloat16)
    stacked = jnp.concatenate([obs_ensemble, obs_values[None], masked[None]], axis=0)
    extended = padded(stacked, (("grid", 1),), REACH)
    chosen = (jnp.arange(dev_blocks, dtype=jnp.int32)[:, None] + REACH + loc_offsets).reshape(-1)
    picked = jnp.take(extended, chosen, axis=1).reshape(local_members + 2, dev_blocks, list_width)
    member_part = picked[:local_members].reshape(local_members, mem_count, per_device, list_width)
    mem_rank = lax.axis_index("mem")
    first_block = mem_rank * per_device
    table_part = lax.dynamic_slice_in_dim(picked[local_members:], first_block, per_device, 1)
    own_taper = lax.dynamic_slice_in_dim(taper_of(loc_offsets), first_block, per_device, 0)
    taper_rows = jnp.repeat(own_taper, slots, axis=1)
    received = lax.all_to_all(member_part, "mem", split_axis=1, concat_axis=0, tiled=True)
    received = received.reshape(MEMBERS, per_device, list_width)
    weight_rows = table_part[1].astype(jnp.float32) * taper_rows
    weights = jax.vmap(block_weights, in_axes=(1, 0, 0))(
        received, table_part[0].astype(jnp.float32), weight_rows
    )
    dev_cols = background.shape[1]
    variables = background.shape[2]
    pieces = background.reshape(local_members, mem_count, per_device * BLOCK_COLS, variables)
    moved = lax.all_to_all(pieces, "mem", split_axis=1, concat_axis=0, tiled=True)
    moved = moved.reshape(MEMBERS, per_device, BLOCK_COLS * variables)
    updated = apply_weights(weights, moved)
    updated = updated.reshape(MEMBERS, 1, per_device * BLOCK_COLS, variables)
    returned = lax.all_to_all(updated, "mem", split_axis=0, concat_axis=1, tiled=True)
    return returned.reshape(local_members, dev_cols, variables)


def solution(mesh):
    placed = (
        P("mem", "grid", None),
        P("grid", None),
        P("grid", None),
        P("grid"),
        P("grid", None),
        P("mem", "grid", None),
    )
    return jax.shard_map(
        on_device, mesh=mesh, in_specs=placed, out_specs=P("mem", "grid", None), check_vma=False
    )
```

profile of v0, /device:TPU:0, one launch (start us, length us, event | category | flops | bytes accessed | tf_op | source)
XLA Modules:
  0.0 82.5 jit_solution(6703048874097502343)
XLA Ops:
  0.0 0.8 fusion.21
  0.8 0.7 copy.22
  1.4 0.9 %copy.21 = bf16[64,4,256]{2,0,1:T(8,128)(2,1)S(1)} copy(bf16[64,4,256]{2,1,0:T(4,128)(2,1)} %param.6) | data formatting | bytes 262144 | tf_op args[0]
  2.4 3.0 %collective-permute-start = (bf16[66,2,256]{2,0,1:T(8,128)(2,1)S(1)}, bf16[66,2,256]{2,0,1:T(8,128)(2,1)S(1)}, u32[]{:S(2)}, u32[]{:S(2)}) collective-permute-start(bf16[66,2,256]{2,0,1:T(8,128)(2,1)S(1)} %get-tuple-element.5), channel_id=1, source_target_pairs={{0,1},{1,2},{2,3},{3,4},{4,5},{5,6},{6,7},{7,0},{8,9},{9,10},{10,1... | collective-permute-start | bytes 202760 | tf_op jit(solution)/shard_map/ppermute | solution.py:20
  5.5 3.1 %collective-permute-start.1 = (bf16[66,2,256]{2,0,1:T(8,128)(2,1)S(1)}, bf16[66,2,256]{2,0,1:T(8,128)(2,1)S(1)}, u32[]{:S(2)}, u32[]{:S(2)}) collective-permute-start(bf16[66,2,256]{2,0,1:T(8,128)(2,1)S(1)} %get-tuple-element.6), channel_id=1, source_target_pairs={{1,0},{2,1},{3,2},{4,3},{5,4},{6,5},{7,6},{0,7},{9,8},{10,9},{11,1... | collective-permute-start | bytes 202760 | tf_op jit(solution)/shard_map/ppermute | solution.py:21
  8.6 0.8 broadcast_add_fusion
  9.5 1.3 %collective-permute-done = bf16[66,2,256]{2,0,1:T(8,128)(2,1)S(1)} collective-permute-done((bf16[66,2,256]{2,0,1:T(8,128)(2,1)S(1)}, bf16[66,2,256]{2,0,1:T(8,128)(2,1)S(1)}, u32[]{:S(2)}, u32[]{:S(2)}) %collective-permute-start) | collective-permute-done | bytes 67616 | tf_op jit(solution)/shard_map/ppermute | solution.py:20
  10.9 0.5 collective-permute-done.1
  11.4 0.6 gather_fusion
  12.7 0.9 %copy.25 = bf16[64,4,1,1024]{3,0,2,1:T(8,128)(2,1)} copy(bf16[64,4,1,1024]{3,1,0,2:T(4,128)(2,1)S(1)} %reshape.380) | data formatting | bytes 1048576 | tf_op jit(solution)/shard_map/reshape | solution.py:72
  13.7 3.5 %all-to-all-start.1 = ((bf16[64,4,1,1024]{3,0,2,1:T(8,128)(2,1)}), bf16[64,4,1,1024]{3,0,2,1:T(8,128)(2,1)S(1)}, u32[]{:S(2)}, u32[]{:S(2)}) async-start(bf16[64,4,1,1024]{3,0,2,1:T(8,128)(2,1)} %copy.25), calls=%async_computation.1 | async-start | bytes 1048576 | tf_op jit(solution)/shard_map/all_to_all | solution.py:78
  17.3 2.7 %copy.20 = bf16[64,4,8,320]{3,2,0,1:T(8,128)(2,1)} copy(bf16[64,4,8,320]{3,2,1,0:T(8,128)(2,1)} %bitcast.102) | data formatting | bytes 2621440 | tf_op jit(solution)/shard_map/reshape | solution.py:86
  20.1 5.9 %all-to-all-done.1 = bf16[64,4,1,1024]{3,0,2,1:T(8,128)(2,1)S(1)} async-done(((bf16[64,4,1,1024]{3,0,2,1:T(8,128)(2,1)}), bf16[64,4,1,1024]{3,0,2,1:T(8,128)(2,1)S(1)}, u32[]{:S(2)}, u32[]{:S(2)}) %all-to-all-start.1) | async-done | bytes 524320 | tf_op jit(solution)/shard_map/all_to_all | solution.py:78
  25.9 3.6 %all-to-all-start = ((bf16[64,4,8,320]{3,2,0,1:T(8,128)(2,1)}), bf16[64,4,8,320]{3,2,0,1:T(8,128)(2,1)S(1)}, u32[]{:S(2)}, u32[]{:S(2)}) async-start(bf16[64,4,8,320]{3,2,0,1:T(8,128)(2,1)} %copy.20), calls=%async_computation | async-start | bytes 3145728 | tf_op jit(solution)/shard_map/all_to_all | solution.py:87
  29.7 0.9 %multiply_reduce_fusion = (f32[]{:T(128)}, f32[256,256]{1,0:T(8,128)S(1)}) fusion(bf16[256,1024]{1,0:T(8,128)(2,1)S(1)} %bitcast.100), kind=kOutput, calls=%fused_computation.34 | convolution fusion | flops 134610944 | bytes 786436 | tf_op jit(solution)/shard_map/vmap()/dot_general | solution.py:35
  31.6 0.4 fusion.15
  32.3 0.4 fusion.7
  33.1 0.4 fusion.26
  33.5 0.4 fusion.6
  34.6 0.4 fusion.5
  35.4 0.4 fusion.30
  35.8 0.4 fusion.4
  36.9 0.4 fusion.3
  37.3 0.5 convolution_bitcast_fusion.2
  37.9 0.4 convolution_divide_fusion
  38.9 10.6 %all-to-all-done = bf16[64,4,8,320]{3,2,0,1:T(8,128)(2,1)S(1)} async-done(((bf16[64,4,8,320]{3,2,0,1:T(8,128)(2,1)}), bf16[64,4,8,320]{3,2,0,1:T(8,128)(2,1)S(1)}, u32[]{:S(2)}, u32[]{:S(2)}) %all-to-all-start) | async-done | bytes 1310752 | tf_op jit(solution)/shard_map/all_to_all | solution.py:87
  49.9 1.9 %convert_bitcast_fusion = f32[4,64,1,8,320]{4,3,1,0,2:T(8,128)} fusion(bf16[64,4,8,320]{3,2,0,1:T(8,128)(2,1)S(1)} %all-to-all-done), kind=kLoop, calls=%fused_computation.3 | loop fusion | flops 655360 | bytes 3932160 | tf_op jit(solution)/shard_map/convert_element_type | solution.py:53
  51.8 2.9 %reshape.383 = f32[256,2560]{1,0:T(8,128)S(1)} reshape(f32[4,64,1,8,320]{4,3,1,0,2:T(8,128)} %convert_bitcast_fusion) | data formatting | bytes 5242880 | tf_op jit(solution)/shard_map/convert_element_type | solution.py:53
  54.7 1.9 %fusion.1 = bf16[1,2560,256]{2,1,0:T(8,128)(2,1)} fusion(f32[256,2560]{1,0:T(8,128)S(1)} %reshape.383, f32[2560]{0:T(1024)S(1)} %div.51, f32[256,256]{1,0:T(8,128)S(1)} %convolution_divide_fusion, f32[256]{0:T(256)S(1)} %broadcast_multiply_fusion.2), kind=kOutput, calls=%fused_computation.5 | convolution fusion | flops 338296832 | bytes 4205568 | tf_op jit(solution)/shard_map/bkj,kbv->jbv/dot_general | solution.py:56
  56.6 2.1 %copy.28 = bf16[256,1,8,320]{3,2,1,0:T(8,128)(2,1)S(1)} copy(bf16[256,1,8,320]{0,3,2,1:T(8,128)(2,1)} %bitcast.99) | data formatting | bytes 2621440 | tf_op jit(solution)/shard_map/reshape | solution.py:90
  58.7 22.5 %all_to_all.33 = bf16[256,1,8,320]{3,2,1,0:T(8,128)(2,1)S(1)} all-to-all(bf16[256,1,8,320]{3,2,1,0:T(8,128)(2,1)S(1)} %copy.28), channel_id=1, replica_groups=mesh['mem'=4,'grid'=8] {'mem'}, dimensions={0} | all-to-all | bytes 2621440 | tf_op jit(solution)/shard_map/all_to_all | solution.py:91
  81.2 1.3 %copy.31 = bf16[64,4,1,8,320]{4,3,1,0,2:T(8,128)(2,1)} copy(bf16[64,4,1,8,320]{4,3,0,1,2:T(8,128)(2,1)S(1)} %bitcast.98) | data formatting | bytes 2621440 | tf_op jit(solution)/shard_map/all_to_all | solution.py:91
  (41 shorter events, 5.1 us)
Async XLA Ops:
  2.4 8.5 %collective-permute-start = (bf16[66,2,256]{2,0,1:T(8,128)(2,1)S(1)}, bf16[66,2,256]{2,0,1:T(8,128)(2,1)S(1)}, u32[]{:S(2)}, u32[]{:S(2)}) collective-permute-start(bf16[66,2,256]{2,0,1:T(8,128)(2,1)S(1)} %get-tuple-element.5), channel_id=1, source_target_pairs={{0,1},{1,2},{2,3},{3,4},{4,5},{5,6},{6,7},{7,0},{8,9},{9,10},{10,1... | collective-permute-start | bytes 202760 | tf_op jit(solution)/shard_map/ppermute | solution.py:20
  5.5 5.9 %collective-permute-start.1 = (bf16[66,2,256]{2,0,1:T(8,128)(2,1)S(1)}, bf16[66,2,256]{2,0,1:T(8,128)(2,1)S(1)}, u32[]{:S(2)}, u32[]{:S(2)}) collective-permute-start(bf16[66,2,256]{2,0,1:T(8,128)(2,1)S(1)} %get-tuple-element.6), channel_id=1, source_target_pairs={{1,0},{2,1},{3,2},{4,3},{5,4},{6,5},{7,6},{0,7},{9,8},{10,9},{11,1... | collective-permute-start | bytes 202760 | tf_op jit(solution)/shard_map/ppermute | solution.py:21
  12.5 4.6 %copy-start = (s32[4,4]{1,0:T(4,128)S(1)}, s32[4,4]{1,0:T(4,128)}, u32[]{:S(2)}) copy-start(s32[4,4]{1,0:T(4,128)} %param.10) | copy-start | bytes 196
  13.7 12.3 %all-to-all-start.1 = ((bf16[64,4,1,1024]{3,0,2,1:T(8,128)(2,1)}), bf16[64,4,1,1024]{3,0,2,1:T(8,128)(2,1)S(1)}, u32[]{:S(2)}, u32[]{:S(2)}) async-start(bf16[64,4,1,1024]{3,0,2,1:T(8,128)(2,1)} %copy.25), calls=%async_computation.1 | async-start | bytes 1048576 | tf_op jit(solution)/shard_map/all_to_all | solution.py:78
  25.9 23.6 %all-to-all-start = ((bf16[64,4,8,320]{3,2,0,1:T(8,128)(2,1)}), bf16[64,4,8,320]{3,2,0,1:T(8,128)(2,1)S(1)}, u32[]{:S(2)}, u32[]{:S(2)}) async-start(bf16[64,4,8,320]{3,2,0,1:T(8,128)(2,1)} %copy.20), calls=%async_computation | async-start | bytes 3145728 | tf_op jit(solution)/shard_map/all_to_all | solution.py:87
where the time goes:
time: 83 us; the launch traced here: 82.5 us
  blocking collectives  22.5 us (27%)
  waiting for transfers between devices  18.4 us (22%)
  starting transfers between devices  13.2 us (16%)
  local copies, waits for them, and re-layouts  13.1 us (16%)
  matrix products  10.2 us (12%)
  other arithmetic  4.13 us (5%)
  between operations  1 us (1%)
    all_to_all x1, blocking collectives, on_device(): lax.all_to_all(updated, 'mem', split_axis=0, concat_axis=1, tiled=True)  22.5 us
    all_to_all x1, waiting for transfers between devices, on_device(): lax.all_to_all(pieces, 'mem', split_axis=1, concat_axis=0, tiled=True)  10.6 us
    all_to_all x1, waiting for transfers between devices, on_device(): lax.all_to_all(member_part, 'mem', split_axis=1, concat_axis=0, tiled=True)  5.87 us
    all_to_all x1, starting transfers between devices, on_device(): lax.all_to_all(pieces, 'mem', split_axis=1, concat_axis=0, tiled=True)  3.56 us
    all_to_all x1, starting transfers between devices, on_device(): lax.all_to_all(member_part, 'mem', split_axis=1, concat_axis=0, tiled=True)  3.47 us
    ppermute x1, starting transfers between devices, padded(): after = lax.ppermute(initial, axis, down)  3.1 us
    ppermute x1, starting transfers between devices, padded(): before = lax.ppermute(last, axis, up)  3.05 us
    convert_element_type x1, local copies, waits for them, and re-layouts, apply_weights(): state_wide = state.astype(jnp.float32)  2.9 us
  transfers between devices with their start and end apart: 4, of which 4 were waited for; matrix products, arithmetic and copies ran while one was open for 15% of the time, Pallas kernels for 0%

commit v1 on v0

--- a/solution.py
+++ b/solution.py
@@ -75,7 +75,9 @@
     table_part = lax.dynamic_slice_in_dim(picked[local_members:], first_block, per_device, 1)
     own_taper = lax.dynamic_slice_in_dim(taper_of(loc_offsets), first_block, per_device, 0)
     taper_rows = jnp.repeat(own_taper, slots, axis=1)
-    received = lax.all_to_all(member_part, "mem", split_axis=1, concat_axis=0, tiled=True)
+    shards = jnp.split(member_part, lax.axis_size("mem"), axis=1)
+    arrived = lax.all_to_all(jnp.stack(shards), "mem", 0, 0)
+    received = jnp.concatenate(arrived, axis=0)
     received = received.reshape(MEMBERS, per_device, list_width)
     weight_rows = table_part[1].astype(jnp.float32) * taper_rows
     weights = jax.vmap(block_weights, in_axes=(1, 0, 0))(

time: 83 us -> 83.8 us (level)
  other arithmetic: 4.13 us -> 4.98 us
    reshape x2 -> x1, local copies, waits for them, and re-layouts: 1.14 us -> 0.2 us  [on_device(): picked[:local_members]]
    another operation x0 -> x1, other arithmetic: none -> 0.86 us  [on_device(): arrived = lax.all_to_all(jnp.stack(shards), 'mem', 0, 0)]
where the time goes in v1:
time: 83.8 us; the launch traced here: 83.3 us
  blocking collectives  22.5 us (27%)
  waiting for transfers between devices  18.1 us (22%)
  starting transfers between devices  13.4 us (16%)
  local copies, waits for them, and re-layouts  13.1 us (16%)
  matrix products  10.2 us (12%)
  other arithmetic  4.98 us (6%)
  between operations  1.07 us (1%)
    all_to_all x1, blocking collectives, on_device(): lax.all_to_all(updated, 'mem', split_axis=0, concat_axis=1, tiled=True)  22.5 us
    all_to_all x1, waiting for transfers between devices, on_device(): lax.all_to_all(pieces, 'mem', split_axis=1, concat_axis=0, tiled=True)  10.4 us
    all_to_all x1, waiting for transfers between devices, on_device(): arrived = lax.all_to_all(jnp.stack(shards), 'mem', 0, 0)  5.87 us
    all_to_all x1, starting transfers between devices, on_device(): lax.all_to_all(pieces, 'mem', split_axis=1, concat_axis=0, tiled=True)  3.74 us
    all_to_all x1, starting transfers between devices, on_device(): arrived = lax.all_to_all(jnp.stack(shards), 'mem', 0, 0)  3.47 us
    ppermute x1, starting transfers between devices, padded(): after = lax.ppermute(initial, axis, down)  3.1 us
    ppermute x1, starting transfers between devices, padded(): before = lax.ppermute(last, axis, up)  3.05 us
    convert_element_type x1, local copies, waits for them, and re-layouts, apply_weights(): state_wide = state.astype(jnp.float32)  2.9 us
  transfers between devices with their start and end apart: 4, of which 4 were waited for; matrix products, arithmetic and copies ran while one was open for 15% of the time, Pallas kernels for 0%

profile of v1, /device:TPU:0, one launch (start us, length us, event | category | flops | bytes accessed | tf_op | source)
XLA Modules:
  0.0 83.3 jit_solution(4463727226949565383)
XLA Ops:
  0.0 0.8 fusion.20
  0.8 0.7 copy.51
  1.4 0.9 %copy.50 = bf16[64,4,256]{2,0,1:T(8,128)(2,1)S(1)} copy(bf16[64,4,256]{2,1,0:T(4,128)(2,1)} %param.6) | data formatting | bytes 262144 | tf_op args[0]
  2.4 3.0 %collective-permute-start = (bf16[66,2,256]{2,0,1:T(8,128)(2,1)S(1)}, bf16[66,2,256]{2,0,1:T(8,128)(2,1)S(1)}, u32[]{:S(2)}, u32[]{:S(2)}) collective-permute-start(bf16[66,2,256]{2,0,1:T(8,128)(2,1)S(1)} %get-tuple-element.9), channel_id=1, source_target_pairs={{0,1},{1,2},{2,3},{3,4},{4,5},{5,6},{6,7},{7,0},{8,9},{9,10},{10,1... | collective-permute-start | bytes 202760 | tf_op jit(solution)/shard_map/ppermute | solution.py:20
  5.5 3.1 %collective-permute-start.1 = (bf16[66,2,256]{2,0,1:T(8,128)(2,1)S(1)}, bf16[66,2,256]{2,0,1:T(8,128)(2,1)S(1)}, u32[]{:S(2)}, u32[]{:S(2)}) collective-permute-start(bf16[66,2,256]{2,0,1:T(8,128)(2,1)S(1)} %get-tuple-element.10), channel_id=1, source_target_pairs={{1,0},{2,1},{3,2},{4,3},{5,4},{6,5},{7,6},{0,7},{9,8},{10,9},{11,1... | collective-permute-start | bytes 202760 | tf_op jit(solution)/shard_map/ppermute | solution.py:21
  8.6 0.8 broadcast_add_fusion
  9.5 1.3 %collective-permute-done = bf16[66,2,256]{2,0,1:T(8,128)(2,1)S(1)} collective-permute-done((bf16[66,2,256]{2,0,1:T(8,128)(2,1)S(1)}, bf16[66,2,256]{2,0,1:T(8,128)(2,1)S(1)}, u32[]{:S(2)}, u32[]{:S(2)}) %collective-permute-start) | collective-permute-done | bytes 67616 | tf_op jit(solution)/shard_map/ppermute | solution.py:20
  10.9 0.5 collective-permute-done.1
  11.4 0.6 gather_fusion
  12.7 0.8 fusion.24
  13.7 0.9 %pad_maximum_fusion = bf16[4,64,1,1,1024]{4,1,3,2,0:T(8,128)(2,1)} fusion(bf16[1,64,1,1,1024]{4,1,3,2,0:T(8,128)(2,1)S(1)} %get-tuple-element.13, bf16[1,64,1,1,1024]{4,1,3,2,0:T(8,128)(2,1)S(1)} %get-tuple-element.14, bf16[1,64,1,1,1024]{4,1,3,2,0:T(8,128)(2,1)S(1)} %get-tuple-element.15, bf16[1,64,1,1,1024]{4,1,3,2,0:T(8,128)(2,1)S(1)} %get-tuple-element.16), kind=kLoop, calls=%fused_computation.31 | loop fusion | flops 786432 | bytes 1048576 | tf_op jit(solution)/shard_map/stack | solution.py:79
  14.5 3.5 %all-to-all-start.1 = ((bf16[4,64,1,1,1024]{4,1,3,2,0:T(8,128)(2,1)}), bf16[4,64,1,1,1024]{4,1,3,2,0:T(8,128)(2,1)S(1)}, u32[]{:S(2)}, u32[]{:S(2)}) async-start(bf16[4,64,1,1,1024]{4,1,3,2,0:T(8,128)(2,1)} %pad_maximum_fusion), calls=%async_computation.1 | async-start | bytes 1048576 | tf_op jit(solution)/shard_map/all_to_all | solution.py:79
  18.1 2.7 %copy.49 = bf16[64,4,8,320]{3,2,0,1:T(8,128)(2,1)} copy(bf16[64,4,8,320]{3,2,1,0:T(8,128)(2,1)} %bitcast.97) | data formatting | bytes 2621440 | tf_op jit(solution)/shard_map/reshape | solution.py:88
  20.9 5.9 %all-to-all-done.1 = bf16[4,64,1,1,1024]{4,1,3,2,0:T(8,128)(2,1)S(1)} async-done(((bf16[4,64,1,1,1024]{4,1,3,2,0:T(8,128)(2,1)}), bf16[4,64,1,1,1024]{4,1,3,2,0:T(8,128)(2,1)S(1)}, u32[]{:S(2)}, u32[]{:S(2)}) %all-to-all-start.1) | async-done | bytes 524320 | tf_op jit(solution)/shard_map/all_to_all | solution.py:79
  26.8 3.7 %all-to-all-start = ((bf16[64,4,8,320]{3,2,0,1:T(8,128)(2,1)}), bf16[64,4,8,320]{3,2,0,1:T(8,128)(2,1)S(1)}, u32[]{:S(2)}, u32[]{:S(2)}) async-start(bf16[64,4,8,320]{3,2,0,1:T(8,128)(2,1)} %copy.49), calls=%async_computation | async-start | bytes 3145728 | tf_op jit(solution)/shard_map/all_to_all | solution.py:89
  30.8 1.0 %multiply_reduce_fusion = (f32[]{:T(128)}, f32[256,256]{1,0:T(8,128)S(1)}) fusion(bf16[256,1024]{1,0:T(8,128)(2,1)S(1)} %bitcast.95), kind=kOutput, calls=%fused_computation.34 | convolution fusion | flops 134610944 | bytes 786436 | tf_op jit(solution)/shard_map/vmap()/dot_general | solution.py:35
  32.7 0.4 fusion.14
  33.4 0.4 fusion.7
  33.8 0.4 fusion.27
  34.2 0.4 fusion.26
  34.6 0.4 fusion.6
  35.7 0.4 fusion.5
  36.9 0.4 fusion.4
  38.1 0.4 fusion.3
  38.4 0.5 convolution_bitcast_fusion.2
  40.0 10.4 %all-to-all-done = bf16[64,4,8,320]{3,2,0,1:T(8,128)(2,1)S(1)} async-done(((bf16[64,4,8,320]{3,2,0,1:T(8,128)(2,1)}), bf16[64,4,8,320]{3,2,0,1:T(8,128)(2,1)S(1)}, u32[]{:S(2)}, u32[]{:S(2)}) %all-to-all-start) | async-done | bytes 1310752 | tf_op jit(solution)/shard_map/all_to_all | solution.py:89
  50.8 1.9 %convert_bitcast_fusion = f32[4,64,1,8,320]{4,3,1,0,2:T(8,128)} fusion(bf16[64,4,8,320]{3,2,0,1:T(8,128)(2,1)S(1)} %all-to-all-done), kind=kLoop, calls=%fused_computation.3 | loop fusion | flops 655360 | bytes 3932160 | tf_op jit(solution)/shard_map/convert_element_type | solution.py:53
  52.6 2.9 %reshape.380 = f32[256,2560]{1,0:T(8,128)S(1)} reshape(f32[4,64,1,8,320]{4,3,1,0,2:T(8,128)} %convert_bitcast_fusion) | data formatting | bytes 5242880 | tf_op jit(solution)/shard_map/convert_element_type | solution.py:53
  55.5 1.9 %fusion.1 = bf16[1,2560,256]{2,1,0:T(8,128)(2,1)} fusion(f32[256,2560]{1,0:T(8,128)S(1)} %reshape.380, f32[2560]{0:T(1024)S(1)} %div.51, f32[256,256]{1,0:T(8,128)S(1)} %convolution_divide_fusion, f32[256]{0:T(256)S(1)} %broadcast_multiply_fusion.2), kind=kOutput, calls=%fused_computation.5 | convolution fusion | flops 338296832 | bytes 4205568 | tf_op jit(solution)/shard_map/bkj,kbv->jbv/dot_general | solution.py:56
  57.4 2.1 %copy.55 = bf16[256,1,8,320]{3,2,1,0:T(8,128)(2,1)S(1)} copy(bf16[256,1,8,320]{0,3,2,1:T(8,128)(2,1)} %bitcast.94) | data formatting | bytes 2621440 | tf_op jit(solution)/shard_map/reshape | solution.py:92
  59.5 22.5 %all_to_all.29 = bf16[256,1,8,320]{3,2,1,0:T(8,128)(2,1)S(1)} all-to-all(bf16[256,1,8,320]{3,2,1,0:T(8,128)(2,1)S(1)} %copy.55), channel_id=1, replica_groups=mesh['mem'=4,'grid'=8] {'mem'}, dimensions={0} | all-to-all | bytes 2621440 | tf_op jit(solution)/shard_map/all_to_all | solution.py:93
  82.0 1.3 %copy.66 = bf16[64,4,1,8,320]{4,3,1,0,2:T(8,128)(2,1)} copy(bf16[64,4,1,8,320]{4,3,0,1,2:T(8,128)(2,1)S(1)} %bitcast.93) | data formatting | bytes 2621440 | tf_op jit(solution)/shard_map/all_to_all | solution.py:93
  (44 shorter events, 5.7 us)
Async XLA Ops:
  2.4 8.5 %collective-permute-start = (bf16[66,2,256]{2,0,1:T(8,128)(2,1)S(1)}, bf16[66,2,256]{2,0,1:T(8,128)(2,1)S(1)}, u32[]{:S(2)}, u32[]{:S(2)}) collective-permute-start(bf16[66,2,256]{2,0,1:T(8,128)(2,1)S(1)} %get-tuple-element.9), channel_id=1, source_target_pairs={{0,1},{1,2},{2,3},{3,4},{4,5},{5,6},{6,7},{7,0},{8,9},{9,10},{10,1... | collective-permute-start | bytes 202760 | tf_op jit(solution)/shard_map/ppermute | solution.py:20
  5.5 5.9 %collective-permute-start.1 = (bf16[66,2,256]{2,0,1:T(8,128)(2,1)S(1)}, bf16[66,2,256]{2,0,1:T(8,128)(2,1)S(1)}, u32[]{:S(2)}, u32[]{:S(2)}) collective-permute-start(bf16[66,2,256]{2,0,1:T(8,128)(2,1)S(1)} %get-tuple-element.10), channel_id=1, source_target_pairs={{1,0},{2,1},{3,2},{4,3},{5,4},{6,5},{7,6},{0,7},{9,8},{10,9},{11,1... | collective-permute-start | bytes 202760 | tf_op jit(solution)/shard_map/ppermute | solution.py:21
  13.6 4.4 %copy-start = (s32[4,4]{1,0:T(4,128)S(1)}, s32[4,4]{1,0:T(4,128)}, u32[]{:S(2)}) copy-start(s32[4,4]{1,0:T(4,128)} %param.10) | copy-start | bytes 196
  14.5 12.3 %all-to-all-start.1 = ((bf16[4,64,1,1,1024]{4,1,3,2,0:T(8,128)(2,1)}), bf16[4,64,1,1,1024]{4,1,3,2,0:T(8,128)(2,1)S(1)}, u32[]{:S(2)}, u32[]{:S(2)}) async-start(bf16[4,64,1,1,1024]{4,1,3,2,0:T(8,128)(2,1)} %pad_maximum_fusion), calls=%async_computation.1 | async-start | bytes 1048576 | tf_op jit(solution)/shard_map/all_to_all | solution.py:79
  26.8 23.6 %all-to-all-start = ((bf16[64,4,8,320]{3,2,0,1:T(8,128)(2,1)}), bf16[64,4,8,320]{3,2,0,1:T(8,128)(2,1)S(1)}, u32[]{:S(2)}, u32[]{:S(2)}) async-start(bf16[64,4,8,320]{3,2,0,1:T(8,128)(2,1)} %copy.49), calls=%async_computation | async-start | bytes 3145728 | tf_op jit(solution)/shard_map/all_to_all | solution.py:89
